TPU v7x, 256 devices: a whole 4x4x8 slice. The times are simulated.
256 devices in a mesh: seq: 32 (over y, x, core), tp: 8 (over z).
Axes of the slice: x: 4, y: 4, z: 8, core: 2. Of those that a mesh axis runs over, the one named last changes fastest.
Arguments:
- tokens: bfloat16 [8192, 4096], P('seq', 'tp'), may hold values from -11 to 11
- grad_out: bfloat16 [8192, 4096], P('seq', 'tp'), may hold values from -1.5 to 1.5
- in_weight: bfloat16 [4096, 4096], P('seq', 'tp'), may hold values from -0.09880682 to 0.09880682
- in_scale: float32 [4096], P('tp'), may hold values from 0.0008238636 to 0.010511364
- out_weight: bfloat16 [4096, 4096], P('seq', 'tp'), may hold values from -0.053943182 to 0.053943182
- out_scale: float32 [4096], replicated, may hold values from 0.00139204545 to 0.0057386364
- state_in: bfloat16 [8192, 128], P('seq'), may hold values from -0.0625 to 0.0625
- state_out: bfloat16 [8192, 128], P('seq'), may hold values from -6 to 6
- log_decay: float32 [8192, 64], P('seq', 'tp'), may hold values from -1.6 to 0
Outputs:
- grad_tokens: bfloat16 [8192, 4096], P('seq', 'tp')
- grad_in_weight: float32 [4096, 4096], P('seq', 'tp')
- grad_in_scale: float32 [4096], P('tp')
- grad_out_weight: float32 [4096, 4096], P('seq', 'tp')
- grad_out_scale: float32 [4096], P('seq')
All inputs are finite; a program needn't handle non-finite values.
Results may differ from a plain program's by a relative error of at most 0.027.
Values may be sent and summed in bfloat16 or wider, within the bound.
No kernel may reach another device: no remote copies, remote signals or barrier semaphores. Data moves between devices by JAX's collectives and lax.ppermute only.
A program may use at most 128 MiB of HBM per device.

v0:
```python
import jax
import jax.numpy as jnp
from jax import lax
from jax.sharding import PartitionSpec as P

D = 4096
HEADS = 64
HEAD_DIM = 64
STRETCH = 256
QMAX = 7
precise = lax.Precision.HIGHEST


def prefix(array, axis, join, neutral, backward):
    count = lax.axis_size(axis)
    place = lax.axis_index(axis)
    ahead = count - 1 - place if backward else place
    gathered = jax.tree.map(
        lambda a, kind: lax.all_gather(a.astype(kind), axis), array, (jnp.bfloat16, jnp.bfloat16)
    )
    state = jax.tree.map(lambda a, e: jnp.zeros_like(a) + jnp.asarray(e, a.dtype), array, neutral)

    def one(turn, state):
        source = count - 1 - turn if backward else turn
        return join(
            state,
            jax.tree.map(
                lambda a, own: lax.dynamic_index_in_dim(a, source, 0, False).astype(own.dtype),
                gathered,
                array,
            ),
        )

    return lax.fori_loop(0, ahead, one, state)


def quantize(weight, channel_scale):
    ratios = weight.astype(jnp.float32) / channel_scale
    clipped = jnp.clip(ratios, -QMAX, QMAX)
    levels = jnp.floor(clipped + 0.5)
    inside = jnp.abs(ratios) <= QMAX
    slopes = jnp.where(inside, levels - ratios, levels)
    return (levels, slopes, inside.astype(jnp.float32))


def stretch_terms(decay_logs, inputs_f, outputs_f):
    cumul = jnp.cumsum(decay_logs, axis=0)
    ending = cumul[-1]
    spread = cumul[:, None, :] - cumul[None, :, :]
    length = decay_logs.shape[0]
    causal = jnp.arange(length)[:, None] >= jnp.arange(length)[None, :]
    mixing = jnp.exp(jnp.where(causal[:, :, None], spread, -jnp.inf))
    intersection = jnp.dot(outputs_f, inputs_f.T, precision=precise)
    return (cumul, ending, mixing * intersection[:, :, None])


def forward_step(carried, pieces):
    values, cumul, ending, weights, inputs_f, outputs_f = pieces
    inner = jnp.einsum("sth,thp->shp", weights, values, precision=precise)
    outer = jnp.exp(cumul)[:, :, None] * jnp.einsum(
        "sn,hnp->shp", outputs_f, carried, precision=precise
    )
    fresh = jnp.einsum(
        "th,tn,thp->hnp", jnp.exp(ending[None, :] - cumul), inputs_f, values, precision=precise
    )
    return (jnp.exp(ending)[:, None, None] * carried + fresh, inner + outer)


def backward_step(carried, pieces):
    grads, cumul, ending, weights, inputs_f, outputs_f = pieces
    inner = jnp.einsum("sth,shp->thp", weights, grads, precision=precise)
    outer = jnp.exp(ending[None, :] - cumul)[:, :, None] * jnp.einsum(
        "tn,hnp->thp", inputs_f, carried, precision=precise
    )
    fresh = jnp.einsum("sh,sn,shp->hnp", jnp.exp(cumul), outputs_f, grads, precision=precise)
    return (jnp.exp(ending)[:, None, None] * carried + fresh, inner + outer)


def join_forward(earlier, later):
    return (earlier[0] * later[0], later[0][:, None, None] * earlier[1] + later[1])


def join_backward(earlier, later):
    return (earlier[0] * later[0], later[1] + later[0][:, None, None] * earlier[1])


def per_device(
    tokens, grad_out, in_weight, in_scale, out_weight, out_scale, state_in, state_out, log_decay
):
    local_rows = tokens.shape[0]
    heads_here = log_decay.shape[1]
    width_here = in_scale.shape[0]
    head_size = width_here // heads_here
    state_size = state_in.shape[1]
    weight_rows = in_weight.shape[0]
    blocks = local_rows // STRETCH
    row_start = lax.axis_index("seq") * weight_rows
    out_scale_rows = lax.dynamic_slice_in_dim(out_scale, row_start, weight_rows)
    in_levels, in_slopes, in_inside = quantize(in_weight, in_scale[None, :])
    out_levels, out_slopes, out_inside = quantize(out_weight, out_scale_rows[:, None])
    in_codes = lax.all_gather(in_levels.astype(jnp.bfloat16), "seq", axis=0, tiled=True)
    out_codes = lax.all_gather(out_levels.astype(jnp.bfloat16), "seq", axis=0, tiled=True)
    features = lax.all_gather(tokens, "tp", axis=1, tiled=True)
    cotangent = lax.all_gather(grad_out, "tp", axis=1, tiled=True)
    projected = jnp.dot(features, in_codes, preferred_element_type=jnp.float32) * in_scale[None, :]
    scaled_grad = (cotangent.astype(jnp.float32) * out_scale[None, :]).astype(jnp.bfloat16)
    grad_mixed = jnp.dot(scaled_grad, out_codes, preferred_element_type=jnp.float32)
    inputs_full = state_in.astype(jnp.float32)
    outputs_full = state_out.astype(jnp.float32)
    decay_blocks = log_decay.reshape(blocks, STRETCH, heads_here)
    input_blocks = inputs_full.reshape(blocks, STRETCH, state_size)
    output_blocks = outputs_full.reshape(blocks, STRETCH, state_size)
    cumul, ending, weights = jax.vmap(stretch_terms)(decay_blocks, input_blocks, output_blocks)
    value_blocks = projected.reshape(blocks, STRETCH, heads_here, head_size)
    grad_blocks = grad_mixed.reshape(blocks, STRETCH, heads_here, head_size)
    empty = jnp.zeros((heads_here, state_size, head_size), jnp.float32)
    local_state, mixed_local = lax.scan(
        forward_step, empty, (value_blocks, cumul, ending, weights, input_blocks, output_blocks)
    )
    local_grad_state, grad_local = lax.scan(
        backward_step,
        empty,
        (grad_blocks, cumul, ending, weights, input_blocks, output_blocks),
        reverse=True,
    )
    running = jnp.cumsum(log_decay, axis=0)
    device_total = running[-1]
    device_decay = jnp.exp(device_total)
    identity = (jnp.ones_like(device_decay), empty)
    entering = prefix((device_decay, local_state), "seq", join_forward, identity, False)[1]
    leaving = prefix((device_decay, local_grad_state), "seq", join_backward, identity, True)[1]
    mixed = mixed_local.reshape(local_rows, heads_here, head_size) + jnp.exp(running)[
        :, :, None
    ] * jnp.einsum("tn,hnp->thp", outputs_full, entering, precision=precise)
    grad_values = grad_local.reshape(local_rows, heads_here, head_size) + jnp.exp(
        device_total[None, :] - running
    )[:, :, None] * jnp.einsum("tn,hnp->thp", inputs_full, leaving, precision=precise)
    mixed = mixed.reshape(local_rows, width_here)
    grad_values = grad_values.reshape(local_rows, width_here)
    mixed_b = mixed.astype(jnp.bfloat16)
    grad_b = grad_values.astype(jnp.bfloat16)
    grad_scaled = (grad_values * in_scale[None, :]).astype(jnp.bfloat16)
    piece = features
    in_total = lax.psum_scatter(
        jnp.einsum("td,tc->dc", piece, grad_b, preferred_element_type=jnp.float32).astype(
            jnp.bfloat16
        ),
        "seq",
        scatter_dimension=0,
        tiled=True,
    ).astype(jnp.float32)
    piece = cotangent
    out_total = lax.psum_scatter(
        jnp.einsum("td,tc->dc", piece, mixed_b, preferred_element_type=jnp.float32).astype(
            jnp.bfloat16
        ),
        "seq",
        scatter_dimension=0,
        tiled=True,
    ).astype(jnp.float32)
    partial_tokens = jnp.einsum(
        "tc,dc->td", grad_scaled, in_codes, preferred_element_type=jnp.float32
    )
    grad_tokens = lax.psum_scatter(
        partial_tokens.astype(jnp.bfloat16), "tp", scatter_dimension=1, tiled=True
    )
    in_part = jnp.sum(in_total * in_slopes, axis=0)
    out_part = jnp.sum(out_total * out_slopes, axis=1)
    in_sum = lax.psum(in_part, "seq")
    out_sum = lax.psum(out_part, "tp")
    grad_in_scale = in_sum / jnp.sqrt(jnp.float32(D * QMAX))
    grad_out_scale = out_sum / jnp.sqrt(jnp.float32(HEADS * HEAD_DIM * QMAX))
    return (
        grad_tokens,
        in_total * in_inside,
        grad_in_scale,
        out_total * out_inside,
        grad_out_scale,
    )


def solution(mesh):
    placed = (
        P("seq", "tp"),
        P("seq", "tp"),
        P("seq", "tp"),
        P("tp"),
        P("seq", "tp"),
        P(),
        P("seq", None),
        P("seq", None),
        P("seq", "tp"),
    )
    return jax.shard_map(
        per_device,
        mesh=mesh,
        in_specs=placed,
        out_specs=(P("seq", "tp"), P("seq", "tp"), P("tp"), P("seq", "tp"), P("seq")),
        check_vma=False,
    )
```

profile of v0, /device:TPU:6, one launch (start us, length us, event | category | flops | bytes accessed | tf_op | source)
XLA Modules:
  0.0 612.6 jit_solution(15400213899961906926)
XLA Ops:
  10.5 1.3 reduce-window.14
  12.4 41.5 %all-gather.10.cloned.1.call-done = bf16[256,4096]{1,0:T(8,128)(2,1)} async-done(((bf16[256,512]{1,0:T(8,128)(2,1)}), bf16[256,4096]{1,0:T(8,128)(2,1)}) %all-gather.10.cloned.1.call-update) | async-done | bytes 2097168 | tf_op jit(solution)/shard_map/all_gather | solution.py:104
  53.9 55.4 %all-gather.12.cloned.1.call-done = bf16[4096,512]{0,1:T(8,128)(2,1)} async-done(((bf16[128,512]{0,1:T(8,128)(2,1)}), bf16[4096,512]{0,1:T(8,128)(2,1)}) %all-gather.12.cloned.1.call-update) | async-done | bytes 4194320 | tf_op jit(solution)/shard_map/all_gather | solution.py:102
  109.3 4.1 fusion.2
  116.2 18.9 %all-gather.2 = bf16[32,1,8]{2,1,0:T(2,128)(2,1)S(1)} all-gather(bf16[1,1,8]{2,1,0:T(2,128)(2,1)S(1)} %bitcast.154), channel_id=1, replica_groups=mesh['seq'=32,'tp'=8] {'seq'}, dimensions={0}, use_global_device_ids=true | all-gather | bytes 528 | tf_op jit(solution)/shard_map/all_gather | solution.py:19
  135.6 1.8 fusion.6
  137.5 28.1 %all-gather.18.cloned.1.call-done = bf16[256,128,64]{1,2,0:T(8,128)(2,1)} async-done(((bf16[8,128,64]{1,2,0:T(8,128)(2,1)}), bf16[256,128,64]{1,2,0:T(8,128)(2,1)}) %all-gather.18.cloned.1.call-update) | async-done | bytes 4194320 | tf_op jit(solution)/shard_map/all_gather | solution.py:19
  165.6 32.6 %while.16 = (s32[]{:T(128)}, f32[8,128,64]{2,1,0:T(8,128)S(1)}, s32[]{:T(128)}, bf16[32,8,128,64]{2,3,1,0:T(8,128)(2,1)}, bf16[32,8]{1,0:T(8,128)(2,1)S(1)}, /*index=5*/s32[]{:T(128)}, s32[]{:T(128)}, s32[]{:T(128)}, s32[]{:T(128)}) while((s32[]{:T(128)}, f32[8,128,64]{2,1,0:T(8,128)S(1)}, s32[]{:T(128)}, bf16[32,8,128,64]{2,3,1,0:T(8,128)(2,1)}, ...), condition=%wide.region_5.6_spmd, body=%wide.region_4.5_spmd.sunk | while | flops 196622 | bytes 1179883 | solution.py:34
  199.3 8.6 %all-gather.16.cloned.1.call-done = bf16[256,4096]{1,0:T(8,128)(2,1)} async-done(((bf16[256,512]{1,0:T(8,128)(2,1)}), bf16[256,4096]{1,0:T(8,128)(2,1)}) %all-gather.16.cloned.1.call-update) | async-done | bytes 2097168 | tf_op jit(solution)/shard_map/all_gather | solution.py:103
  207.9 4.8 fusion
  212.7 6.5 %copy.81 = bf16[4096,512]{1,0:T(8,128)(2,1)} copy(bf16[4096,512]{0,1:T(8,128)(2,1)} %fusion) | data formatting | bytes 8388608
  220.2 87.2 %reduce-scatter.10.cloned.1.call-done = bf16[128,512]{1,0:T(8,128)(2,1)} async-done(((bf16[4096,512]{1,0:T(8,128)(2,1)}), bf16[128,512]{1,0:T(8,128)(2,1)}) %reduce-scatter.10.cloned.1.call-update) | async-done | bytes 131088
  309.3 54.8 %all-gather.14.cloned.1.call-done = bf16[4096,512]{0,1:T(8,128)(2,1)} async-done(((bf16[128,512]{0,1:T(8,128)(2,1)}), bf16[4096,512]{0,1:T(8,128)(2,1)}) %all-gather.14.cloned.1.call-update) | async-done | bytes 4194320 | tf_op jit(solution)/shard_map/all_gather | solution.py:101
  364.1 3.5 convolution_multiply_fusion
  369.6 3.5 fusion.7
  373.0 47.4 %all-gather.20.cloned.1.call-done = bf16[256,128,64]{1,2,0:T(8,128)(2,1)} async-done(((bf16[8,128,64]{1,2,0:T(8,128)(2,1)}), bf16[256,128,64]{1,2,0:T(8,128)(2,1)}) %all-gather.20.cloned.1.call-update) | async-done | bytes 4194320 | tf_op jit(solution)/shard_map/all_gather | solution.py:19
  420.5 8.0 %while.17 = (s32[]{:T(128)}, f32[8,128,64]{2,1,0:T(8,128)S(1)}, s32[]{:T(128)}, bf16[32,8]{1,0:T(8,128)(2,1)S(1)}, bf16[32,8,128,64]{2,3,1,0:T(8,128)(2,1)}, /*index=5*/s32[]{:T(128)}, s32[]{:T(128)}, s32[]{:T(128)}) while((s32[]{:T(128)}, f32[8,128,64]{2,1,0:T(8,128)S(1)}, s32[]{:T(128)}, bf16[32,8]{1,0:T(8,128)(2,1)S(1)}, ...), condition=%wide.region_11.12_spmd, body=%wide.region_10.11_spmd.sunk | while | flops 196621 | bytes 1179863 | solution.py:34
  430.1 3.2 fusion.1
  433.4 6.5 %copy.83 = bf16[4096,512]{1,0:T(8,128)(2,1)} copy(bf16[4096,512]{0,1:T(8,128)(2,1)} %fusion.1) | data formatting | bytes 8388608
  440.1 4.9 convolution_convert_fusion.2
  445.8 83.4 %psum.14 = f32[512]{0:T(512)S(1)} all-reduce(f32[512]{0:T(512)S(1)} %get-tuple-element.273), channel_id=1, replica_groups=mesh['seq'=32,'tp'=8] {'seq'}, use_global_device_ids=true, to_apply=%region_9.10 | all-reduce | flops 512 | bytes 4096 | tf_op jit(solution)/shard_map/psum | solution.py:169
  529.8 31.0 %reduce-scatter.12.cloned.1.call-done = bf16[128,512]{1,0:T(8,128)(2,1)} async-done(((bf16[4096,512]{1,0:T(8,128)(2,1)}), bf16[128,512]{1,0:T(8,128)(2,1)}) %reduce-scatter.12.cloned.1.call-update) | async-done | bytes 131088
  562.8 17.4 %psum.15 = f32[128]{0:T(128)S(1)} all-reduce(f32[128]{0:T(128)S(1)} %get-tuple-element.275), channel_id=1, replica_groups=mesh['seq'=32,'tp'=8] {'tp'}, use_global_device_ids=true, to_apply=%region_14.15 | all-reduce | flops 128 | bytes 1024 | tf_op jit(solution)/shard_map/psum | solution.py:170
  580.7 25.3 %reduce-scatter.8.cloned.1.call-done = bf16[256,512]{1,0:T(8,128)(2,1)} async-done(((bf16[256,4096]{1,0:T(8,128)(2,1)}), bf16[256,512]{1,0:T(8,128)(2,1)}) %reduce-scatter.8.cloned.1.call-update) | async-done | bytes 262160 | tf_op jit(solution)/shard_map/reduce_scatter | solution.py:164
  (203 shorter events, 58.0 us)
Async XLA Ops:
  7.2 128.3 %copy-start = (bf16[256,128]{1,0:T(8,128)(2,1)S(1)}, bf16[256,128]{1,0:T(8,128)(2,1)}, u32[]{:S(2)}) copy-start(bf16[256,128]{1,0:T(8,128)(2,1)} %param.19) | copy-start | bytes 196612
  7.2 46.7 %all-gather.10.cloned.1.call-start = ((), (), s32[]{:S(2)}) async-start(), calls=%async_computation.3 | async-start | bytes 2359296 | tf_op jit(solution)/shard_map/all_gather | solution.py:104
  7.9 101.4 %all-gather.12.cloned.1.call-start = ((), (), s32[]{:S(2)}) async-start(), calls=%async_computation.4 | async-start | bytes 4325376 | tf_op jit(solution)/shard_map/all_gather | solution.py:102
  10.5 155.0 %all-gather.18.cloned.1.call-start = ((), (), s32[]{:S(2)}) async-start(), calls=%async_computation.8 | async-start | bytes 4325376 | tf_op jit(solution)/shard_map/all_gather | solution.py:19
  12.4 101.1 %copy-start.3 = (bf16[256,128]{1,0:T(8,128)(2,1)S(1)}, bf16[256,128]{1,0:T(8,128)(2,1)}, u32[]{:S(2)}) copy-start(bf16[256,128]{1,0:T(8,128)(2,1)} %param.20) | copy-start | bytes 196612
  12.4 102.8 %copy-start.8 = (f32[256,8]{0,1:T(8,128)S(1)}, f32[256,8]{0,1:T(8,128)}, u32[]{:S(2)}) copy-start(f32[256,8]{0,1:T(8,128)} %param.21) | copy-start | bytes 24580
  114.5 93.4 %all-gather.16.cloned.1.call-start = ((), (), s32[]{:S(2)}) async-start(), calls=%async_computation.7 | async-start | bytes 2359296 | tf_op jit(solution)/shard_map/all_gather | solution.py:103
  115.1 192.3 %reduce-scatter.10.cloned.1.call-start = ((), (), s32[]{:S(2)}) async-start(), calls=%async_computation.10 | async-start | bytes 4325376
  135.6 30.0 %copy-start.5 = (f32[256,256]{1,0:T(8,128)}, f32[256,256]{1,0:T(8,128)S(1)}, u32[]{:S(2)}) copy-start(f32[256,256]{1,0:T(8,128)S(1)} %fusion.57) | copy-start | bytes 786436
  219.2 0.9 copy-start.7
  219.2 89.2 %copy-start.9 = (f32[512]{0:T(512)S(1)}, f32[512]{0:T(512)}, u32[]{:S(2)}) copy-start(f32[512]{0:T(512)} %param.16) | copy-start | bytes 6148
  219.2 145.0 %copy-start.2 = (bf16[256,4096]{1,0:T(8,128)(2,1)S(1)}, bf16[256,4096]{1,0:T(8,128)(2,1)}, u32[]{:S(2)}) copy-start(bf16[256,4096]{1,0:T(8,128)(2,1)} %all-gather.16.cloned.1.call-done) | copy-start | bytes 6291460
  219.2 145.0 %all-gather.14.cloned.1.call-start = ((), (), s32[]{:S(2)}) async-start(), calls=%async_computation.5 | async-start | bytes 4325376 | tf_op jit(solution)/shard_map/all_gather | solution.py:101
  309.3 60.3 %copy-start.6 = (f32[256,256]{1,0:T(8,128)S(1)}, f32[256,256]{1,0:T(8,128)}, u32[]{:S(2)}) copy-start(f32[256,256]{1,0:T(8,128)} %copy-done.5) | copy-start | bytes 786436
  309.3 111.2 %all-gather.20.cloned.1.call-start = ((), (), s32[]{:S(2)}) async-start(), calls=%async_computation.9 | async-start | bytes 4325376 | tf_op jit(solution)/shard_map/all_gather | solution.py:19
  367.6 0.8 copy-start.4
  369.5 191.3 %reduce-scatter.12.cloned.1.call-start = ((), (), s32[]{:S(2)}) async-start(), calls=%async_computation.11 | async-start | bytes 4325376
  428.5 1.6 copy-start.1
  439.9 166.1 %reduce-scatter.8.cloned.1.call-start = ((), (), s32[]{:S(2)}) async-start(), calls=%async_computation.6 | async-start | bytes 2359296 | tf_op jit(solution)/shard_map/reduce_scatter | solution.py:164
Sparse Core Ops, SparseCore 0:
  9.8 44.0 all-gather.9
  56.9 52.3 all-gather.11
  114.6 50.8 all-gather.17
  167.2 40.6 all-gather.15
  219.3 88.0 reduce-scatter.9
  310.6 53.5 all-gather.13
  369.6 50.7 all-gather.19
  440.0 120.7 reduce-scatter.11
  563.9 42.0 reduce-scatter.7
where the time goes:
time: 614 us; the launch traced here: 613 us
  waiting for transfers between devices  381 us (62%)
  blocking collectives  120 us (20%)
  local copies, waits for them, and re-layouts  55.6 us (9%)
  matrix products  30.2 us (5%)
  between operations  14.1 us (2%)
  other arithmetic  10.6 us (2%)
    unnamed x11, waiting for transfers between devices  119 us
    psum x1, blocking collectives, per_device(): in_sum = lax.psum(in_part, 'seq')  83.4 us
    all_gather x2, waiting for transfers between devices, prefix(): lax.all_gather(a.astype(kind), axis)  75.5 us
    all_gather x1, waiting for transfers between devices, per_device(): lax.all_gather(out_levels.astype(jnp.bfloat16), 'seq', axis=0, tiled=True)  55.4 us
    all_gather x1, waiting for transfers between devices, per_device(): lax.all_gather(in_levels.astype(jnp.bfloat16), 'seq', axis=0, tiled=True)  54.8 us
    all_gather x1, waiting for transfers between devices, per_device(): cotangent = lax.all_gather(grad_out, 'tp', axis=1, tiled=True)  41.5 us
    dynamic_slice x62, local copies, waits for them, and re-layouts, one(): lax.dynamic_index_in_dim(a, source, 0, False).astype(own.dtype)  34 us
    reduce_scatter x1, waiting for transfers between devices, per_device(): lax.psum_scatter(partial_tokens.astype(jnp.bfloat16), 'tp', scatter_dimen...  25.3 us
  transfers between devices with their start and end apart: 9, of which 9 were waited for; matrix products, arithmetic and copies ran while one was open for 9% of the time, Pallas kernels for 0%

commit v1 on v0

--- a/solution.py
+++ b/solution.py
@@ -167,7 +167,14 @@
     in_part = jnp.sum(in_total * in_slopes, axis=0)
     out_part = jnp.sum(out_total * out_slopes, axis=1)
     in_sum = lax.psum(in_part, "seq")
-    out_sum = lax.psum(out_part, "tp")
+    fan = lax.axis_size("tp")
+    out_sum, o_now = (out_part, 0)
+    while 1 << o_now < fan:
+        left_arr = lax.ppermute(
+            out_sum, "tp", perm=[(dev_i, dev_i ^ 1 << o_now) for dev_i in range(fan)]
+        )
+        out_sum = out_sum + left_arr
+        o_now = o_now + 1
     grad_in_scale = in_sum / jnp.sqrt(jnp.float32(D * QMAX))
     grad_out_scale = out_sum / jnp.sqrt(jnp.float32(HEADS * HEAD_DIM * QMAX))
     return (

time: 614 us -> 646 us (1.052)
  the two profiles are of different devices: /device:TPU:6 before, /device:TPU:1 now
where the time goes in v1:
time: 646 us; the launch traced here: 645 us
  waiting for transfers between devices  439 us (68%)
  blocking collectives  86.3 us (13%)
  local copies, waits for them, and re-layouts  55.6 us (9%)
  matrix products  30.2 us (5%)
  between operations  14.1 us (2%)
  other arithmetic  10.6 us (2%)
  starting transfers between devices  7.72 us (1%)
    unnamed x11, waiting for transfers between devices  209 us
    all_gather x2, waiting for transfers between devices, prefix(): lax.all_gather(a.astype(kind), axis)  73.6 us
    psum x1, blocking collectives, per_device(): in_sum = lax.psum(in_part, 'seq')  65.8 us
    all_gather x1, waiting for transfers between devices, per_device(): lax.all_gather(out_levels.astype(jnp.bfloat16), 'seq', axis=0, tiled=True)  60 us
    all_gather x1, waiting for transfers between devices, per_device(): lax.all_gather(in_levels.astype(jnp.bfloat16), 'seq', axis=0, tiled=True)  57 us
    all_gather x1, waiting for transfers between devices, per_device(): cotangent = lax.all_gather(grad_out, 'tp', axis=1, tiled=True)  38.7 us
    dynamic_slice x62, local copies, waits for them, and re-layouts, one(): lax.dynamic_index_in_dim(a, source, 0, False).astype(own.dtype)  34 us
    all_gather x1, blocking collectives, prefix(): lax.all_gather(a.astype(kind), axis)  20.6 us
  transfers between devices with their start and end apart: 12, of which 9 were waited for; matrix products, arithmetic and copies ran while one was open for 9% of the time, Pallas kernels for 0%

profile of v1, /device:TPU:1, one launch (start us, length us, event | category | flops | bytes accessed | tf_op | source)
XLA Modules:
  0.0 645.2 jit_solution(15842385427275647314)
XLA Ops:
  10.5 1.3 reduce-window.14
  12.4 38.7 %all-gather.10.cloned.1.call-done = bf16[256,4096]{1,0:T(8,128)(2,1)} async-done(((bf16[256,512]{1,0:T(8,128)(2,1)}), bf16[256,4096]{1,0:T(8,128)(2,1)}) %all-gather.10.cloned.1.call-update) | async-done | bytes 2097168 | tf_op jit(solution)/shard_map/all_gather | solution.py:104
  51.1 60.0 %all-gather.12.cloned.1.call-done = bf16[4096,512]{0,1:T(8,128)(2,1)} async-done(((bf16[128,512]{0,1:T(8,128)(2,1)}), bf16[4096,512]{0,1:T(8,128)(2,1)}) %all-gather.12.cloned.1.call-update) | async-done | bytes 4194320 | tf_op jit(solution)/shard_map/all_gather | solution.py:102
  111.1 4.1 fusion.2
  118.0 20.6 %all-gather.2 = bf16[32,1,8]{2,1,0:T(2,128)(2,1)S(1)} all-gather(bf16[1,1,8]{2,1,0:T(2,128)(2,1)S(1)} %bitcast.154), channel_id=1, replica_groups=mesh['seq'=32,'tp'=8] {'seq'}, dimensions={0}, use_global_device_ids=true | all-gather | bytes 528 | tf_op jit(solution)/shard_map/all_gather | solution.py:19
  139.0 1.8 fusion.6
  140.9 26.3 %all-gather.18.cloned.1.call-done = bf16[256,128,64]{1,2,0:T(8,128)(2,1)} async-done(((bf16[8,128,64]{1,2,0:T(8,128)(2,1)}), bf16[256,128,64]{1,2,0:T(8,128)(2,1)}) %all-gather.18.cloned.1.call-update) | async-done | bytes 4194320 | tf_op jit(solution)/shard_map/all_gather | solution.py:19
  167.2 39.1 %while.16 = (s32[]{:T(128)}, f32[8,128,64]{2,1,0:T(8,128)S(1)}, s32[]{:T(128)}, bf16[32,8,128,64]{2,3,1,0:T(8,128)(2,1)}, bf16[32,8]{1,0:T(8,128)(2,1)S(1)}, /*index=5*/s32[]{:T(128)}, s32[]{:T(128)}, s32[]{:T(128)}, s32[]{:T(128)}) while((s32[]{:T(128)}, f32[8,128,64]{2,1,0:T(8,128)S(1)}, s32[]{:T(128)}, bf16[32,8,128,64]{2,3,1,0:T(8,128)(2,1)}, ...), condition=%wide.region_5.6_spmd, body=%wide.region_4.5_spmd.sunk | while | flops 196622 | bytes 1179883 | solution.py:34
  207.5 4.8 fusion
  212.3 6.5 copy.81
  219.8 87.1 %reduce-scatter.10.cloned.1.call-done = bf16[128,512]{1,0:T(8,128)(2,1)} async-done(((bf16[4096,512]{1,0:T(8,128)(2,1)}), bf16[128,512]{1,0:T(8,128)(2,1)}) %reduce-scatter.10.cloned.1.call-update) | async-done | bytes 131088
  308.9 57.0 %all-gather.14.cloned.1.call-done = bf16[4096,512]{0,1:T(8,128)(2,1)} async-done(((bf16[128,512]{0,1:T(8,128)(2,1)}), bf16[4096,512]{0,1:T(8,128)(2,1)}) %all-gather.14.cloned.1.call-update) | async-done | bytes 4194320 | tf_op jit(solution)/shard_map/all_gather | solution.py:101
  365.9 3.5 convolution_multiply_fusion
  371.3 3.5 fusion.7
  374.7 47.3 %all-gather.20.cloned.1.call-done = bf16[256,128,64]{1,2,0:T(8,128)(2,1)} async-done(((bf16[8,128,64]{1,2,0:T(8,128)(2,1)}), bf16[256,128,64]{1,2,0:T(8,128)(2,1)}) %all-gather.20.cloned.1.call-update) | async-done | bytes 4194320 | tf_op jit(solution)/shard_map/all_gather | solution.py:19
  422.1 1.5 while.17
  425.2 3.2 fusion.1
  428.4 6.5 %copy.83 = bf16[4096,512]{1,0:T(8,128)(2,1)} copy(bf16[4096,512]{0,1:T(8,128)(2,1)} %fusion.1) | data formatting | bytes 8388608
  435.1 4.8 convolution_convert_fusion.2
  440.0 120.1 %reduce-scatter.12.cloned.1.call-done = bf16[128,512]{1,0:T(8,128)(2,1)} async-done(((bf16[4096,512]{1,0:T(8,128)(2,1)}), bf16[128,512]{1,0:T(8,128)(2,1)}) %reduce-scatter.12.cloned.1.call-update) | async-done | bytes 131088
  561.3 1.4 collective-permute-start
  563.8 2.3 collective-permute-start.1
  566.0 65.8 %psum.7 = f32[512]{0:T(512)S(1)} all-reduce(f32[512]{0:T(512)S(1)} %get-tuple-element.273), channel_id=1, replica_groups=mesh['seq'=32,'tp'=8] {'seq'}, use_global_device_ids=true, to_apply=%region_9.10 | all-reduce | flops 512 | bytes 4096 | tf_op jit(solution)/shard_map/psum | solution.py:169
  631.8 3.7 collective-permute-start.2
  (210 shorter events, 59.5 us)
Async XLA Ops:
  7.2 131.7 %copy-start = (bf16[256,128]{1,0:T(8,128)(2,1)S(1)}, bf16[256,128]{1,0:T(8,128)(2,1)}, u32[]{:S(2)}) copy-start(bf16[256,128]{1,0:T(8,128)(2,1)} %param.19) | copy-start | bytes 196612
  7.2 43.9 %all-gather.10.cloned.1.call-start = ((), (), s32[]{:S(2)}) async-start(), calls=%async_computation.3 | async-start | bytes 2359296 | tf_op jit(solution)/shard_map/all_gather | solution.py:104
  7.9 103.2 %all-gather.12.cloned.1.call-start = ((), (), s32[]{:S(2)}) async-start(), calls=%async_computation.4 | async-start | bytes 4325376 | tf_op jit(solution)/shard_map/all_gather | solution.py:102
  10.5 156.7 %all-gather.18.cloned.1.call-start = ((), (), s32[]{:S(2)}) async-start(), calls=%async_computation.8 | async-start | bytes 4325376 | tf_op jit(solution)/shard_map/all_gather | solution.py:19
  12.4 102.8 %copy-start.3 = (bf16[256,128]{1,0:T(8,128)(2,1)S(1)}, bf16[256,128]{1,0:T(8,128)(2,1)}, u32[]{:S(2)}) copy-start(bf16[256,128]{1,0:T(8,128)(2,1)} %param.20) | copy-start | bytes 196612
  12.4 104.5 %copy-start.8 = (f32[256,8]{0,1:T(8,128)S(1)}, f32[256,8]{0,1:T(8,128)}, u32[]{:S(2)}) copy-start(f32[256,8]{0,1:T(8,128)} %param.21) | copy-start | bytes 24580
  116.3 91.2 %all-gather.16.cloned.1.call-start = ((), (), s32[]{:S(2)}) async-start(), calls=%async_computation.7 | async-start | bytes 2359296 | tf_op jit(solution)/shard_map/all_gather | solution.py:103
  116.9 190.0 %reduce-scatter.10.cloned.1.call-start = ((), (), s32[]{:S(2)}) async-start(), calls=%async_computation.10 | async-start | bytes 4325376
  139.0 28.2 %copy-start.5 = (f32[256,256]{1,0:T(8,128)}, f32[256,256]{1,0:T(8,128)S(1)}, u32[]{:S(2)}) copy-start(f32[256,256]{1,0:T(8,128)S(1)} %fusion.57) | copy-start | bytes 786436
  218.7 0.9 copy-start.7
  218.8 89.2 %copy-start.9 = (f32[512]{0:T(512)S(1)}, f32[512]{0:T(512)}, u32[]{:S(2)}) copy-start(f32[512]{0:T(512)} %param.16) | copy-start | bytes 6148
  218.8 147.1 %copy-start.2 = (bf16[256,4096]{1,0:T(8,128)(2,1)S(1)}, bf16[256,4096]{1,0:T(8,128)(2,1)}, u32[]{:S(2)}) copy-start(bf16[256,4096]{1,0:T(8,128)(2,1)} %all-gather.16.cloned.1.call-done) | copy-start | bytes 6291460
  218.8 147.1 %all-gather.14.cloned.1.call-start = ((), (), s32[]{:S(2)}) async-start(), calls=%async_computation.5 | async-start | bytes 4325376 | tf_op jit(solution)/shard_map/all_gather | solution.py:101
  308.8 62.5 %copy-start.6 = (f32[256,256]{1,0:T(8,128)S(1)}, f32[256,256]{1,0:T(8,128)}, u32[]{:S(2)}) copy-start(f32[256,256]{1,0:T(8,128)} %copy-done.5) | copy-start | bytes 786436
  308.8 113.2 %all-gather.20.cloned.1.call-start = ((), (), s32[]{:S(2)}) async-start(), calls=%async_computation.9 | async-start | bytes 4325376 | tf_op jit(solution)/shard_map/all_gather | solution.py:19
  369.3 0.8 copy-start.4
  371.2 188.9 %reduce-scatter.12.cloned.1.call-start = ((), (), s32[]{:S(2)}) async-start(), calls=%async_computation.11 | async-start | bytes 4325376
  423.6 1.6 copy-start.1
  435.0 203.8 %reduce-scatter.8.cloned.1.call-start = ((), (), s32[]{:S(2)}) async-start(), calls=%async_computation.6 | async-start | bytes 2359296 | tf_op jit(solution)/shard_map/reduce_scatter | solution.py:164
  561.3 2.5 collective-permute-start
  563.8 68.0 %collective-permute-start.1 = (f32[128]{0:T(128)S(1)}, f32[128]{0:T(128)S(1)}, u32[]{:S(2)}, u32[]{:S(2)}) collective-permute-start(f32[128]{0:T(128)S(1)} %add.102), channel_id=1, source_target_pairs={{0,2},{1,3},{2,0},{3,1},{4,6},{5,7},{6,4},{7,5},{8,10},{9,11},{10,... | collective-permute-start | bytes 1544 | tf_op jit(solution)/shard_map/ppermute | solution.py:173
  631.8 6.4 collective-permute-start.2
Sparse Core Ops, SparseCore 0:
  9.8 41.2 all-gather.9
  54.1 56.9 all-gather.11
  116.4 50.7 all-gather.17
  168.8 36.9 all-gather.15
  218.9 87.9 reduce-scatter.9
  310.1 55.6 all-gather.13
  371.3 50.6 all-gather.19
  435.1 125.0 reduce-scatter.11
  563.3 38.8 reduce-scatter.7
